TPU v7x, 256 devices: a whole 4x4x8 slice. The times are simulated.
256 devices in a mesh: grp: 16 (over x_lo, z), inner: 16 (over y, x_hi, core).
Axes of the slice: x: 4 (x_hi: 2, x_lo: 2; x = x_hi * 2 + x_lo), y: 4, z: 8, core: 2. Of those that a mesh axis runs over, the one named last changes fastest.
Arguments:
- signal: bfloat16 [128, 1024, 4096], P('grp', None, 'inner'), may hold values from -6 to 6
- bins: int32 [8], replicated, may hold values from 1 to 512, as said below
- mic_positions: float32 [3, 4096], replicated, may hold values from -1 to 1
- grid_positions: float32 [3, 1024], replicated, may hold values from 1 to 3
Outputs:
- beam_map: float32 [8, 1024], replicated
Inputs may be any that keep to these rules, and one draw needn't show every extreme that they name: The 8 bins are distinct; bin 1 and bin 1024 / 2 are always among them.
All inputs are finite; a program needn't handle non-finite values.
Results may differ from a plain program's by a relative error of at most 0.02.
Values may be sent and summed in bfloat16 or wider, within the bound.
A program may use at most 128 MiB of HBM per device.

v0:
```python
import math

import jax
import jax.numpy as jnp
from jax import lax
from jax.sharding import PartitionSpec as P

SAMPLES = 1024
F = 8


TWO_PI = 2.0 * math.pi
RATE_OVER_SOUND = 51200.0 / 343.0


def dft_table(bins):
    ticks = jnp.arange(SAMPLES, dtype=jnp.int32)
    turns = bins[:, None] * ticks[None, :] % SAMPLES
    angle = turns.astype(jnp.float32) * (TWO_PI / SAMPLES)
    window = 0.5 - 0.5 * jnp.cos(ticks.astype(jnp.float32) * (TWO_PI / SAMPLES))
    factor = math.sqrt(8.0 / (3.0 * SAMPLES))
    real_part = window[None, :] * jnp.cos(angle) * factor
    imag_part = -window[None, :] * jnp.sin(angle) * factor
    return jnp.concatenate([real_part, imag_part], 0).astype(jnp.bfloat16)


def distances(spots, grid):
    delta_x = grid[0][None, :] - spots[0][:, None]
    delta_y = grid[1][None, :] - spots[1][:, None]
    delta_z = grid[2][None, :] - spots[2][:, None]
    return jnp.sqrt(delta_x * delta_x + delta_y * delta_y + delta_z * delta_z) * RATE_OVER_SOUND


def steering(delay, frequency_bin):
    angle = delay * (frequency_bin.astype(jnp.float32) * (TWO_PI / SAMPLES))
    return jnp.concatenate([jnp.cos(angle), -jnp.sin(angle)], 0).astype(jnp.bfloat16)


def shards(signal, bins, mic_positions, grid_positions):
    table = dft_table(bins)
    local = jnp.einsum("kt,stm->skm", table, signal, preferred_element_type=jnp.float32).astype(
        jnp.bfloat16
    )
    snap_dev = local.shape[0]
    mic_cols = local.shape[2]
    local = local.reshape(snap_dev, 2, F, mic_cols)
    grp_size = lax.axis_size("grp")
    grp_index = lax.axis_index("grp")
    inner_index = lax.axis_index("inner")
    total_mics = mic_positions.shape[1]
    snaps = snap_dev * grp_size
    col_pos = lax.dynamic_slice_in_dim(mic_positions, inner_index * mic_cols, mic_cols, 1)
    col_delay = distances(col_pos, grid_positions)
    wide = lax.all_gather(local, "inner", axis=3, tiled=True)
    rows = lax.all_to_all(wide, "grp", split_axis=3, concat_axis=0, tiled=True)
    row_count = rows.shape[3]
    row_ids = grp_index * row_count + jnp.arange(row_count, dtype=jnp.int32)
    row_pos = lax.dynamic_slice_in_dim(mic_positions, grp_index * row_count, row_count, 1)
    col_ids = inner_index * mic_cols + jnp.arange(mic_cols, dtype=jnp.int32)
    row_delay = distances(row_pos, grid_positions)
    piece = lax.all_gather(local, "grp", axis=0, tiled=True)
    real_rows = rows[:, 0]
    imag_rows = rows[:, 1]
    real_cols = piece[:, 0]
    imag_cols = piece[:, 1]
    form = "sfm,sfn->fmn"
    real_sum = jnp.einsum(
        form, real_rows, real_cols, preferred_element_type=jnp.float32
    ) + jnp.einsum(form, imag_rows, imag_cols, preferred_element_type=jnp.float32)
    imag_sum = jnp.einsum(
        form, imag_rows, real_cols, preferred_element_type=jnp.float32
    ) - jnp.einsum(form, real_rows, imag_cols, preferred_element_type=jnp.float32)
    diagonal_mask = row_ids[:, None] == col_ids[None, :]
    partial_value = []
    for index in range(F):
        real_c = jnp.where(diagonal_mask, 0.0, real_sum[index] / snaps)
        imag_c = jnp.where(diagonal_mask, 0.0, imag_sum[index] / snaps)
        block = jnp.concatenate(
            [jnp.concatenate([real_c, -imag_c], 1), jnp.concatenate([imag_c, real_c], 1)], 0
        )
        col_steer = steering(col_delay, bins[index]).astype(jnp.float32)
        row_steer = steering(row_delay, bins[index]).astype(jnp.float32)
        image = jnp.dot(
            block, col_steer, precision=lax.Precision.HIGHEST, preferred_element_type=jnp.float32
        )
        partial_value.append(jnp.sum(row_steer * image, axis=0))
    partial_value = jnp.stack(partial_value, 0)
    total = lax.psum(partial_value, ("grp", "inner"))
    return total * (math.sqrt(snaps) / total_mics)


def solution(mesh):
    in_specs = (P("grp", None, "inner"), P(), P(), P())
    out_specs = P()
    return jax.shard_map(shards, mesh=mesh, in_specs=in_specs, out_specs=out_specs, check_vma=False)
```

profile of v0, /device:TPU:1, one launch (start us, length us, event | category | flops | bytes accessed | tf_op | source)
XLA Modules:
  0.0 348.1 jit_solution(14160871644973293209)
XLA Ops:
  6.6 0.9 multiply_convert_fusion.1
  7.5 3.5 fusion
  11.0 0.7 all-gather.5.cloned.1.call-update
  11.7 51.2 %all-gather.3.cloned.1.call-done = bf16[8,2,8,4096]{3,2,1,0:T(8,128)(2,1)} async-done(((bf16[8,2,8,256]{3,2,1,0:T(8,128)(2,1)}), bf16[8,2,8,4096]{3,2,1,0:T(8,128)(2,1)}) %all-gather.3.cloned.1.call-update) | async-done | bytes 1048592 | tf_op jit(solution)/shard_map/all_gather | solution.py:54
  62.9 32.9 %copy.11 = bf16[8,2,8,4096]{2,1,0,3:T(2,128)(2,1)} copy(bf16[8,2,8,4096]{3,2,1,0:T(8,128)(2,1)} %all-gather.3.cloned.1.call-done) | data formatting | bytes 2097152 | tf_op jit(solution)/shard_map/all_gather | solution.py:54
  95.8 20.6 %reshape.88 = bf16[16,2,16384]{2,1,0:T(2,128)(2,1)} reshape(bf16[4096,8,2,8]{3,2,1,0:T(2,128)(2,1)} %bitcast.129) | data formatting | bytes 2097152
  116.5 7.0 %all-to-all-start = ((bf16[16,2,16384]{2,1,0:T(2,128)(2,1)}), bf16[16,2,16384]{2,1,0:T(2,128)(2,1)S(1)}, u32[]{:S(2)}, u32[]{:S(2)}) async-start(bf16[16,2,16384]{2,1,0:T(2,128)(2,1)} %reshape.88), calls=%async_computation | async-start | bytes 2097152 | tf_op jit(solution)/shard_map/all_to_all | solution.py:55
  123.5 0.7 fusion.139
  129.3 0.9 constant_dynamic-slice_fusion.1
  130.2 66.2 %cosine_convert_fusion = (bf16[256,1024]{1,0:T(8,128)(2,1)}, bf16[256,1024]{1,0:T(8,128)(2,1)S(1)}, bf16[256,1024]{1,0:T(8,128)(2,1)}, bf16[256,1024]{1,0:T(8,12...) fusion(f32[]{:T(128)} %bitcast.49, ...), kind=kLoop, calls=%fused_computation.109 | loop fusion | flops 20971520 | bytes 16795680 | tf_op jit(solution)/shard_map/convert
  196.5 1.3 fusion.137
  198.6 20.8 %reshape.89 = bf16[4096,8,2,8]{3,2,1,0:T(2,128)(2,1)} reshape(bf16[16,2,16384]{2,1,0:T(2,128)(2,1)S(1)} %all-to-all-done) | data formatting | bytes 2097152
  219.4 24.9 %copy.12 = bf16[8,2,8,16,256]{4,0,3,2,1:T(8,128)(2,1)S(1)} copy(bf16[8,2,8,16,256]{2,1,0,4,3:T(2,128)(2,1)} %bitcast.130) | data formatting | bytes 2097152 | tf_op jit(solution)/shard_map/all_to_all | solution.py:55
  246.1 0.8 fusion.129
  247.5 1.9 multiply_reduce_fusion.1
  249.6 1.9 multiply_reduce_fusion.2
  251.6 1.9 multiply_reduce_fusion.3
  253.6 1.9 multiply_reduce_fusion.4
  255.7 1.9 multiply_reduce_fusion.5
  257.7 2.2 multiply_reduce_fusion.6
  260.0 1.9 multiply_reduce_fusion
  261.9 1.9 multiply_reduce_fusion.7
  263.9 76.7 %psum.7 = f32[8,1024]{1,0:T(8,128)S(1)} all-reduce(f32[8,1024]{1,0:T(8,128)S(1)} %stack.35), channel_id=1, replica_groups=mesh['grp'=16,'inner'=16] {'grp','inner'}, use_global_device_ids=true, to_apply=%region_8.9 | all-reduce | flops 8192 | bytes 65536 | tf_op jit(solution)/shard_map/psum | solution.py:88
  340.6 0.6 broadcast_multiply_fusion
  (81 shorter events, 3.5 us)
Async XLA Ops:
  6.5 56.4 %all-gather.3.cloned.1.call-start = ((), (), s32[]{:S(2)}) async-start(), calls=%async_computation.1 | async-start | bytes 1114112 | tf_op jit(solution)/shard_map/all_gather | solution.py:54
  11.0 185.5 %all-gather.5.cloned.1.call-start = ((), (), s32[]{:S(2)}) async-start(), calls=%async_computation.2 | async-start | bytes 1114112 | tf_op jit(solution)/shard_map/all_gather | solution.py:61
  116.5 7.0 %copy-start = (s32[8]{0:T(128)S(1)}, s32[8]{0:T(128)}, u32[]{:S(2)}) copy-start(s32[8]{0:T(128)} %param.5) | copy-start | bytes 100
  116.5 13.7 %copy-start.1 = (f32[3,1024]{1,0:T(4,128)S(1)}, f32[3,1024]{1,0:T(4,128)}, u32[]{:S(2)}) copy-start(f32[3,1024]{1,0:T(4,128)} %param.7) | copy-start | bytes 36868
  116.5 82.2 %all-to-all-start = ((bf16[16,2,16384]{2,1,0:T(2,128)(2,1)}), bf16[16,2,16384]{2,1,0:T(2,128)(2,1)S(1)}, u32[]{:S(2)}, u32[]{:S(2)}) async-start(bf16[16,2,16384]{2,1,0:T(2,128)(2,1)} %reshape.88), calls=%async_computation | async-start | bytes 2097152 | tf_op jit(solution)/shard_map/all_to_all | solution.py:55
  249.5 2.0 copy-start.21
  249.5 2.0 copy-start.22
  249.6 2.0 copy-start.23
  249.6 2.0 copy-start.24
  251.6 2.0 copy-start.17
  251.6 2.0 copy-start.18
  251.6 2.0 copy-start.19
  251.6 2.0 copy-start.20
  255.6 2.0 copy-start.9
  255.6 2.0 copy-start.10
  255.6 2.0 copy-start.11
  255.6 2.0 copy-start.12
  257.6 2.2 copy-start.5
  257.7 2.2 copy-start.6
  257.7 2.2 copy-start.7
  257.7 2.2 copy-start.8
  259.9 2.0 copy-start.2
  259.9 2.0 copy-start.3
  259.9 2.0 copy-start.4
  (12 other events, 20.9 us)
Sparse Core Ops, SparseCore 0:
  11.1 51.7 all-gather.2
  64.7 57.6 all-gather.4
where the time goes:
time: 353 us; the launch traced here: 348 us
  local copies, waits for them, and re-layouts  104 us (29%)
  blocking collectives  76.7 us (22%)
  other arithmetic  68.6 us (19%)
  waiting for transfers between devices  51.9 us (15%)
  matrix products  20.9 us (6%)
  between operations  19.1 us (5%)
  starting transfers between devices  7.02 us (2%)
    psum x1, blocking collectives, shards(): total = lax.psum(partial_value, ('grp', 'inner'))  76.7 us
    another operation x2, other arithmetic  67.1 us
    all_gather x1, waiting for transfers between devices, shards(): wide = lax.all_gather(local, 'inner', axis=3, tiled=True)  51.2 us
    unnamed x70, local copies, waits for them, and re-layouts  43 us
    all_gather x1, local copies, waits for them, and re-layouts, shards(): wide = lax.all_gather(local, 'inner', axis=3, tiled=True)  32.9 us
    all_to_all x1, local copies, waits for them, and re-layouts, shards(): rows = lax.all_to_all(wide, 'grp', split_axis=3, concat_axis=0, tiled=True)  24.9 us
    dot_general x8, matrix products, shards(): jnp.dot(block, col_steer, precision=lax.Precision.HIGHEST, preferred_elem...  15.8 us
  transfers between devices with their start and end apart: 3, of which 1 were waited for; matrix products, arithmetic and copies ran while one was open for 35% of the time, Pallas kernels for 0%

commit v1 on v0

v1 whole, which is shorter than its diff:
```python
import functools
import math

import jax
import jax.numpy as jnp
from jax import lax
from jax.experimental import pallas as pl
from jax.experimental.pallas import tpu as pltpu
from jax.sharding import PartitionSpec as P

SAMPLES = 1024
F = 8
X_LO = 2
TURNS_PER_METRE = (51200.0 / 343.0) / SAMPLES
MESH = pl.DeviceIdType.MESH

COS = (
    1.0,
    -19.73920440673828,
    64.93911743164062,
    -85.45014190673828,
    60.16762924194336,
    -25.967599868774414,
    6.528658390045166,
)
SIN = (
    6.283185005187988,
    -41.341590881347656,
    81.59994506835938,
    -76.61447143554688,
    41.3428840637207,
    -12.471243858337402,
)


def horner(coefficients, u):
    value = jnp.full_like(u, coefficients[-1])
    for coefficient in coefficients[-2::-1]:
        value = value * u + coefficient
    return value


def cos_sin(turns):
    r = turns - jnp.round(turns)
    u = r * r
    return horner(COS, u), r * horner(SIN, u)


def kernel(
    groups,
    inners,
    total_mics,
    bins_ref,
    signal_hbm,
    mic_hbm,
    grid_hbm,
    out_ref,
    signal,
    mic,
    grid,
    grid_cols,
    wide,
    spectra,
    received,
    cos_st,
    sin_st,
    excess,
    share,
    shares,
    value,
    values,
    signal_sem,
    mic_sem,
    grid_sem,
    x_send,
    x_recv,
    a_send,
    a_recv,
    b_send,
    b_recv,
):
    depth = groups // X_LO
    plane = X_LO * inners
    splits = plane // F
    snaps = signal.shape[0]
    mics = signal.shape[2]
    points = grid.shape[1]
    part = points // splits

    me_g = lax.axis_index("grp")
    me_i = lax.axis_index("inner")
    me_x = me_g // depth
    me_z = me_g % depth
    me_q = me_i * X_LO + me_x
    me_f = me_q // splits
    me_p = me_q % splits

    plane_peers = []
    for di in range(inners):
        for dx in range(X_LO):
            if di or dx:
                x = (me_x + dx) % X_LO
                i = (me_i + di) % inners
                plane_peers.append((x * depth + me_z, i, i * X_LO + x))
    depth_peers = [(me_x * depth + (me_z + dz) % depth, me_i) for dz in range(1, depth)]

    loads = []
    for s in range(snaps):
        loads.append(pltpu.make_async_copy(signal_hbm.at[s], signal.at[s], signal_sem.at[s]))
    for load in loads:
        load.start()
    grid_load = pltpu.make_async_copy(grid_hbm, grid, grid_sem)
    mic_load = pltpu.make_async_copy(mic_hbm, mic, mic_sem)
    grid_load.start()
    mic_load.start()

    barrier = pltpu.get_barrier_semaphore()
    for g, i, _ in plane_peers:
        pl.semaphore_signal(barrier, inc=1, device_id=(g, i), device_id_type=MESH)
    for g, i in depth_peers:
        pl.semaphore_signal(barrier, inc=1, device_id=(g, i), device_id_type=MESH)

    row = lax.broadcasted_iota(jnp.int32, (F, SAMPLES), 0)
    tick = lax.broadcasted_iota(jnp.int32, (F, SAMPLES), 1)
    bin_rows = jnp.zeros((F, SAMPLES), jnp.int32)
    for f in range(F):
        bin_rows = jnp.where(row == f, bins_ref[f], bin_rows)
    turns = lax.rem(bin_rows * tick, SAMPLES).astype(jnp.float32) * (1.0 / SAMPLES)
    cos_w, _ = cos_sin(tick.astype(jnp.float32) * (1.0 / SAMPLES))
    window = (0.5 - 0.5 * cos_w) * math.sqrt(8.0 / (3.0 * SAMPLES))
    cos_t, sin_t = cos_sin(turns)
    table = jnp.concatenate([window * cos_t, -(window * sin_t)], 0).astype(jnp.bfloat16)

    for s in range(snaps):
        loads[s].wait()
        wide[:, s, :] = jnp.dot(table, signal[s], preferred_element_type=jnp.float32)
    for f in range(F):
        spectra[f] = jnp.concatenate([wide[f], wide[F + f]], 0).astype(jnp.bfloat16)

    pl.semaphore_wait(barrier, len(plane_peers) + len(depth_peers))
    for g, i, q in plane_peers:
        pltpu.make_async_remote_copy(
            src_ref=spectra.at[q // splits],
            dst_ref=received.at[me_q],
            send_sem=x_send,
            recv_sem=x_recv,
            device_id=(g, i),
            device_id_type=MESH,
        ).start()
    pltpu.make_async_copy(spectra.at[me_f], received.at[me_q], x_recv).start()

    grid_load.wait()
    for axis in range(3):
        for tile in range(part // 128):
            at = pl.multiple_of(me_p * part + tile * 128, 128)
            line = grid[pl.ds(axis, 1), pl.ds(at, 128)]
            grid_cols[axis, pl.ds(tile * 128, 128), :] = jnp.transpose(
                jnp.broadcast_to(line, (128, 128))
            )
    mic_load.wait()
    rate = bins_ref[me_f].astype(jnp.float32) * TURNS_PER_METRE
    rows = 32

    def steer_block(block, carry):
        for tile in range(mics // 128):
            at = pl.multiple_of(block * mics + tile * 128, 128)
            mic_x = jnp.broadcast_to(mic[pl.ds(0, 1), pl.ds(at, 128)], (rows, 128))
            mic_y = jnp.broadcast_to(mic[pl.ds(1, 1), pl.ds(at, 128)], (rows, 128))
            mic_z = jnp.broadcast_to(mic[pl.ds(2, 1), pl.ds(at, 128)], (rows, 128))
            across = pl.ds(tile * 128, 128)
            for first in range(0, part, rows):
                down = pl.ds(first, rows)
                dx = grid_cols[0, down, :] - mic_x
                dy = grid_cols[1, down, :] - mic_y
                dz = grid_cols[2, down, :] - mic_z
                cos_a, sin_a = cos_sin(jnp.sqrt(dx * dx + dy * dy + dz * dz) * rate)
                cos_b = cos_a.astype(jnp.bfloat16)
                sin_b = sin_a.astype(jnp.bfloat16)
                cos_st[block, down, across] = cos_b
                sin_st[block, down, across] = sin_b
                cos_r = cos_b.astype(jnp.float32)
                sin_r = sin_b.astype(jnp.float32)
                excess[block, down, across] = (
                    (cos_r * cos_r - 1.0) + sin_r * sin_r
                ).astype(jnp.bfloat16)
        return carry

    lax.fori_loop(0, inners, steer_block, 0)

    pltpu.make_async_copy(received, received, x_recv).wait()

    lines = 2 * X_LO * snaps
    contract = (((1,), (1,)), ((), ()))

    def beam_block(block, carry):
        by_cos, by_sin, by_excess, energy = carry
        x = received[pl.ds(block * X_LO, X_LO)].reshape(lines, mics)
        wide_x = x.astype(jnp.float32)
        power = jnp.sum(wide_x * wide_x, axis=0, keepdims=True)
        power_b = jnp.broadcast_to(power, (16, mics)).astype(jnp.bfloat16)
        by_cos += lax.dot_general(x, cos_st[block], contract, preferred_element_type=jnp.float32)
        by_sin += lax.dot_general(x, sin_st[block], contract, preferred_element_type=jnp.float32)
        by_excess += lax.dot_general(
            power_b, excess[block], contract, preferred_element_type=jnp.float32
        )
        return by_cos, by_sin, by_excess, energy + power

    by_cos, by_sin, by_excess, energy = lax.fori_loop(
        0,
        inners,
        beam_block,
        (
            jnp.zeros((lines, part), jnp.float32),
            jnp.zeros((lines, part), jnp.float32),
            jnp.zeros((16, part), jnp.float32),
            jnp.zeros((1, mics), jnp.float32),
        ),
    )
    total = jnp.zeros((1, part), jnp.float32)
    for x in range(X_LO):
        re = slice(2 * x * snaps, (2 * x + 1) * snaps)
        im = slice((2 * x + 1) * snaps, (2 * x + 2) * snaps)
        beam_r = by_cos[re] - by_sin[im]
        beam_i = by_cos[im] + by_sin[re]
        total += jnp.sum(beam_r * beam_r + beam_i * beam_i, axis=0, keepdims=True)
    total -= jnp.sum(energy, axis=1, keepdims=True) + by_excess[0:1]

    halves = part // 128
    for h in range(halves):
        share[h : h + 1, :] = total[:, h * 128 : (h + 1) * 128]
    for g, i in depth_peers:
        pltpu.make_async_remote_copy(
            src_ref=share,
            dst_ref=shares.at[me_z],
            send_sem=a_send,
            recv_sem=a_recv,
            device_id=(g, i),
            device_id_type=MESH,
        ).start()
    shares[me_z] = share[...]
    pltpu.make_async_copy(
        shares.at[pl.ds(0, depth - 1)], shares.at[pl.ds(0, depth - 1)], a_recv
    ).wait()

    scale = 1.0 / (math.sqrt(groups * snaps) * total_mics)
    value[...] = jnp.sum(shares[...], axis=0) * scale
    for g, i, _ in plane_peers:
        pltpu.make_async_remote_copy(
            src_ref=value,
            dst_ref=values.at[me_q],
            send_sem=b_send,
            recv_sem=b_recv,
            device_id=(g, i),
            device_id_type=MESH,
        ).start()
    values[me_q] = value[...]
    pltpu.make_async_copy(
        values.at[pl.ds(0, plane - 1)], values.at[pl.ds(0, plane - 1)], b_recv
    ).wait()
    for q in range(plane):
        for h in range(halves):
            at = (q % splits) * part + h * 128
            out_ref[q // splits : q // splits + 1, at : at + 128] = values[q, h : h + 1, :]

    pltpu.make_async_copy(
        received.at[pl.ds(0, plane - 1)], received.at[pl.ds(0, plane - 1)], x_send
    ).wait()
    pltpu.make_async_copy(
        shares.at[pl.ds(0, depth - 1)], shares.at[pl.ds(0, depth - 1)], a_send
    ).wait()
    pltpu.make_async_copy(
        values.at[pl.ds(0, plane - 1)], values.at[pl.ds(0, plane - 1)], b_send
    ).wait()


def shards(groups, inners, signal, bins, mic_positions, grid_positions):
    snaps, _, mics = signal.shape
    total_mics = mic_positions.shape[1]
    points = grid_positions.shape[1]
    plane = X_LO * inners
    part = points // (plane // F)
    halves = part // 128
    bf16, f32 = jnp.bfloat16, jnp.float32
    dma = pltpu.SemaphoreType.DMA
    return pl.pallas_call(
        functools.partial(kernel, groups, inners, total_mics),
        out_shape=jax.ShapeDtypeStruct((F, points), f32),
        in_specs=[
            pl.BlockSpec(memory_space=pltpu.SMEM),
            pl.BlockSpec(memory_space=pltpu.HBM),
            pl.BlockSpec(memory_space=pltpu.HBM),
            pl.BlockSpec(memory_space=pltpu.HBM),
        ],
        out_specs=pl.BlockSpec(memory_space=pltpu.VMEM),
        scratch_shapes=[
            pltpu.VMEM(signal.shape, bf16),
            pltpu.VMEM(mic_positions.shape, f32),
            pltpu.VMEM(grid_positions.shape, f32),
            pltpu.VMEM((3, part, 128), f32),
            pltpu.VMEM((2 * F, snaps, mics), f32),
            pltpu.VMEM((F, 2 * snaps, mics), bf16),
            pltpu.VMEM((plane, 2 * snaps, mics), bf16),
            pltpu.VMEM((inners, part, mics), bf16),
            pltpu.VMEM((inners, part, mics), bf16),
            pltpu.VMEM((inners, part, mics), bf16),
            pltpu.VMEM((halves, 128), f32),
            pltpu.VMEM((groups // X_LO, halves, 128), f32),
            pltpu.VMEM((halves, 128), f32),
            pltpu.VMEM((plane, halves, 128), f32),
            dma((snaps,)),
        ]
        + [dma] * 8,
        compiler_params=pltpu.CompilerParams(
            collective_id=0, has_side_effects=True, vmem_limit_bytes=67_043_328
        ),
        name="beamform",
    )(bins, signal, mic_positions, grid_positions)


def solution(mesh):
    in_specs = (P("grp", None, "inner"), P(), P(), P())
    body = functools.partial(shards, mesh.shape["grp"], mesh.shape["inner"])
    return jax.shard_map(body, mesh=mesh, in_specs=in_specs, out_specs=P(), check_vma=False)
```

time: 353 us -> 35.2 us (0.10); the launches traced: 348 us -> 35.1 us
  local copies, waits for them, and re-layouts: 104 us -> 1.38 us
  blocking collectives: 76.7 us -> 0 us
  other arithmetic: 68.6 us -> 0 us
  waiting for transfers between devices: 51.9 us -> 0 us
  Pallas kernels: 0 us -> 33.7 us
  matrix products: 20.9 us -> 0 us
  between operations: 19.1 us -> 0.01 us
  starting transfers between devices: 7.02 us -> 0 us
    psum x1 -> x0, blocking collectives: 76.7 us -> none  [shards(): total = lax.psum(partial_value, ('grp', 'inner'))]
    another operation x2 -> x0, other arithmetic: 67.1 us -> none
    all_gather x2 -> x0, waiting for transfers between devices: 51.2 us -> none  [the longest x1 51.2 us: shards(): wide = lax.all_gather(local, 'inner', axis=3, tiled=True)]
    unnamed x70 -> x1, local copies, waits for them, and re-layouts: 43 us -> 1.38 us
    pallas_call x0 -> x1, Pallas kernels: none -> 33.7 us  [shards(): pl.pallas_call(functools.partial(kernel, groups, inners, total_mics), out...]
    all_gather x1 -> x0, local copies, waits for them, and re-layouts: 32.9 us -> none  [shards(): wide = lax.all_gather(local, 'inner', axis=3, tiled=True)]
    all_to_all x1 -> x0, local copies, waits for them, and re-layouts: 24.9 us -> none  [shards(): rows = lax.all_to_all(wide, 'grp', split_axis=3, concat_axis=0, tiled=True)]
    dot_general x13 -> x0, matrix products: 20.9 us -> none  [the longest x8 15.8 us: shards(): jnp.dot(block, col_steer, precision=lax.Precision.HIGHEST, preferred_elem...]
  transfers between devices with their start and end apart: 3 -> 0, of which waited for: 1 -> 0; matrix products, arithmetic and copies ran while one was open for 35% -> 0% of each run, Pallas kernels for 0% -> 0%
where the time goes in v1:
time: 35.2 us; the launch traced here: 35.1 us
  Pallas kernels  33.7 us (96%)
  local copies, waits for them, and re-layouts  1.38 us (4%)
    pallas_call x1, Pallas kernels, shards(): pl.pallas_call(functools.partial(kernel, groups, inners, total_mics), out...  33.7 us
    unnamed x1, local copies, waits for them, and re-layouts  1.38 us

profile of v1, /device:TPU:1, one launch (start us, length us, event | category | flops | bytes accessed | tf_op | source)
XLA Modules:
  0.0 35.1 jit_solution(2463324414560891613)
XLA Ops:
  0.0 33.7 %beamform.1 = f32[8,1024]{1,0:T(8,128)} custom-call(s32[8]{0:T(128)} %bins_ref.1, bf16[8,1024,256]{2,1,0:T(8,128)(2,1)} %signal_hbm.1, f32[3,4096]{1,0:T(4,128)} %mic_hbm.1, f32[3,1024]{1,0:T(4,128)} %grid_hbm.1), custom_call_target="tpu_custom_call" | custom-call | tf_op jit(solution)/shard_map/beamform/pallas_call | solution.py:285
  33.7 1.4 %copy.6 = f32[8,1024]{1,0:T(8,128)} copy(f32[8,1024]{1,0:T(8,128)} %beamform.1) | data formatting | bytes 65536

commit v2 on v1

--- a/solution.py
+++ b/solution.py
@@ -50,11 +50,12 @@
     groups,
     inners,
     total_mics,
-    bins_ref,
+    bins_hbm,
     signal_hbm,
     mic_hbm,
     grid_hbm,
     out_ref,
+    bins_ref,
     signal,
     mic,
     grid,
@@ -69,6 +70,7 @@
     shares,
     value,
     values,
+    bins_sem,
     signal_sem,
     mic_sem,
     grid_sem,
@@ -95,15 +97,32 @@
     me_f = me_q // splits
     me_p = me_q % splits
 
+    me_c = me_i % 2
+    me_h = me_i // 2 % 2
+    me_y = me_i // 4
+    ys = inners // 4
     plane_peers = []
-    for di in range(inners):
-        for dx in range(X_LO):
-            if di or dx:
-                x = (me_x + dx) % X_LO
-                i = (me_i + di) % inners
-                plane_peers.append((x * depth + me_z, i, i * X_LO + x))
-    depth_peers = [(me_x * depth + (me_z + dz) % depth, me_i) for dz in range(1, depth)]
-
+    near, far = [], []
+    for dy in range(ys):
+        for dh in range(2):
+            hops = min(dy, ys - dy) + (2 if dh else 1)
+            for dc in range(2):
+                i = (me_y + dy) % ys * 4 + (me_h + dh) % 2 * 2 + (me_c + dc) % 2
+                (far if hops > 2 else near).append(i)
+                for dx in range(X_LO):
+                    if dy or dh or dc or dx:
+                        x = (me_x + dx) % X_LO
+                        away = min(dy, ys - dy) + (2 - dx if dh else dx)
+                        plane_peers.append(
+                            (away + dc, x * depth + me_z, i, i * X_LO + x, int(hops > 2))
+                        )
+    plane_peers.sort(key=lambda peer: -peer[0])
+    plane_peers = [peer[1:] for peer in plane_peers]
+    steps = sorted(range(1, depth), key=lambda dz: -min(dz, depth - dz))
+    depth_peers = [(me_x * depth + (me_z + dz) % depth, me_i) for dz in steps]
+
+    bins_load = pltpu.make_async_copy(bins_hbm, bins_ref, bins_sem)
+    bins_load.start()
     loads = []
     for s in range(snaps):
         loads.append(pltpu.make_async_copy(signal_hbm.at[s], signal.at[s], signal_sem.at[s]))
@@ -115,13 +134,14 @@
     mic_load.start()
 
     barrier = pltpu.get_barrier_semaphore()
-    for g, i, _ in plane_peers:
+    for g, i, _, _ in plane_peers:
         pl.semaphore_signal(barrier, inc=1, device_id=(g, i), device_id_type=MESH)
     for g, i in depth_peers:
         pl.semaphore_signal(barrier, inc=1, device_id=(g, i), device_id_type=MESH)
 
     row = lax.broadcasted_iota(jnp.int32, (F, SAMPLES), 0)
     tick = lax.broadcasted_iota(jnp.int32, (F, SAMPLES), 1)
+    bins_load.wait()
     bin_rows = jnp.zeros((F, SAMPLES), jnp.int32)
     for f in range(F):
         bin_rows = jnp.where(row == f, bins_ref[f], bin_rows)
@@ -138,42 +158,43 @@
         spectra[f] = jnp.concatenate([wide[f], wide[F + f]], 0).astype(jnp.bfloat16)
 
     pl.semaphore_wait(barrier, len(plane_peers) + len(depth_peers))
-    for g, i, q in plane_peers:
+    for g, i, q, late in plane_peers:
         pltpu.make_async_remote_copy(
             src_ref=spectra.at[q // splits],
             dst_ref=received.at[me_q],
             send_sem=x_send,
-            recv_sem=x_recv,
+            recv_sem=x_recv.at[late],
             device_id=(g, i),
             device_id_type=MESH,
         ).start()
-    pltpu.make_async_copy(spectra.at[me_f], received.at[me_q], x_recv).start()
-
+    pltpu.make_async_copy(spectra.at[me_f], received.at[me_q], x_recv.at[0]).start()
+
+    rate = bins_ref[me_f].astype(jnp.float32) * TURNS_PER_METRE
     grid_load.wait()
     for axis in range(3):
         for tile in range(part // 128):
             at = pl.multiple_of(me_p * part + tile * 128, 128)
-            line = grid[pl.ds(axis, 1), pl.ds(at, 128)]
+            line = grid[pl.ds(axis, 1), pl.ds(at, 128)] * rate
             grid_cols[axis, pl.ds(tile * 128, 128), :] = jnp.transpose(
                 jnp.broadcast_to(line, (128, 128))
             )
     mic_load.wait()
-    rate = bins_ref[me_f].astype(jnp.float32) * TURNS_PER_METRE
     rows = 32
 
     def steer_block(block, carry):
         for tile in range(mics // 128):
             at = pl.multiple_of(block * mics + tile * 128, 128)
-            mic_x = jnp.broadcast_to(mic[pl.ds(0, 1), pl.ds(at, 128)], (rows, 128))
-            mic_y = jnp.broadcast_to(mic[pl.ds(1, 1), pl.ds(at, 128)], (rows, 128))
-            mic_z = jnp.broadcast_to(mic[pl.ds(2, 1), pl.ds(at, 128)], (rows, 128))
+            mic_x = jnp.broadcast_to(mic[pl.ds(0, 1), pl.ds(at, 128)] * rate, (rows, 128))
+            mic_y = jnp.broadcast_to(mic[pl.ds(1, 1), pl.ds(at, 128)] * rate, (rows, 128))
+            mic_z = jnp.broadcast_to(mic[pl.ds(2, 1), pl.ds(at, 128)] * rate, (rows, 128))
             across = pl.ds(tile * 128, 128)
             for first in range(0, part, rows):
                 down = pl.ds(first, rows)
                 dx = grid_cols[0, down, :] - mic_x
                 dy = grid_cols[1, down, :] - mic_y
                 dz = grid_cols[2, down, :] - mic_z
-                cos_a, sin_a = cos_sin(jnp.sqrt(dx * dx + dy * dy + dz * dz) * rate)
+                squared = jnp.maximum(dx * dx + dy * dy + dz * dz, 1e-30)
+                cos_a, sin_a = cos_sin(squared * lax.rsqrt(squared))
                 cos_b = cos_a.astype(jnp.bfloat16)
                 sin_b = sin_a.astype(jnp.bfloat16)
                 cos_st[block, down, across] = cos_b
@@ -187,35 +208,31 @@
 
     lax.fori_loop(0, inners, steer_block, 0)
 
-    pltpu.make_async_copy(received, received, x_recv).wait()
-
     lines = 2 * X_LO * snaps
     contract = (((1,), (1,)), ((), ()))
-
-    def beam_block(block, carry):
-        by_cos, by_sin, by_excess, energy = carry
-        x = received[pl.ds(block * X_LO, X_LO)].reshape(lines, mics)
-        wide_x = x.astype(jnp.float32)
-        power = jnp.sum(wide_x * wide_x, axis=0, keepdims=True)
-        power_b = jnp.broadcast_to(power, (16, mics)).astype(jnp.bfloat16)
-        by_cos += lax.dot_general(x, cos_st[block], contract, preferred_element_type=jnp.float32)
-        by_sin += lax.dot_general(x, sin_st[block], contract, preferred_element_type=jnp.float32)
-        by_excess += lax.dot_general(
-            power_b, excess[block], contract, preferred_element_type=jnp.float32
-        )
-        return by_cos, by_sin, by_excess, energy + power
-
-    by_cos, by_sin, by_excess, energy = lax.fori_loop(
-        0,
-        inners,
-        beam_block,
-        (
-            jnp.zeros((lines, part), jnp.float32),
-            jnp.zeros((lines, part), jnp.float32),
-            jnp.zeros((16, part), jnp.float32),
-            jnp.zeros((1, mics), jnp.float32),
-        ),
-    )
+    by_cos = jnp.zeros((lines, part), jnp.float32)
+    by_sin = jnp.zeros((lines, part), jnp.float32)
+    by_excess = jnp.zeros((16, part), jnp.float32)
+    energy = jnp.zeros((1, mics), jnp.float32)
+    for late, blocks in enumerate((near, far)):
+        if blocks:
+            landed = received.at[pl.ds(0, X_LO * len(blocks))]
+            pltpu.make_async_copy(landed, landed, x_recv.at[late]).wait()
+        for block in blocks:
+            x = received[pl.ds(block * X_LO, X_LO)].reshape(lines, mics)
+            wide_x = x.astype(jnp.float32)
+            power = jnp.sum(wide_x * wide_x, axis=0, keepdims=True)
+            power_b = jnp.broadcast_to(power, (16, mics)).astype(jnp.bfloat16)
+            by_cos += lax.dot_general(
+                x, cos_st[block], contract, preferred_element_type=jnp.float32
+            )
+            by_sin += lax.dot_general(
+                x, sin_st[block], contract, preferred_element_type=jnp.float32
+            )
+            by_excess += lax.dot_general(
+                power_b, excess[block], contract, preferred_element_type=jnp.float32
+            )
+            energy += power
     total = jnp.zeros((1, part), jnp.float32)
     for x in range(X_LO):
         re = slice(2 * x * snaps, (2 * x + 1) * snaps)
@@ -244,7 +261,7 @@
 
     scale = 1.0 / (math.sqrt(groups * snaps) * total_mics)
     value[...] = jnp.sum(shares[...], axis=0) * scale
-    for g, i, _ in plane_peers:
+    for g, i, _, _ in plane_peers:
         pltpu.make_async_remote_copy(
             src_ref=value,
             dst_ref=values.at[me_q],
@@ -286,13 +303,14 @@
         functools.partial(kernel, groups, inners, total_mics),
         out_shape=jax.ShapeDtypeStruct((F, points), f32),
         in_specs=[
-            pl.BlockSpec(memory_space=pltpu.SMEM),
+            pl.BlockSpec(memory_space=pltpu.HBM),
             pl.BlockSpec(memory_space=pltpu.HBM),
             pl.BlockSpec(memory_space=pltpu.HBM),
             pl.BlockSpec(memory_space=pltpu.HBM),
         ],
         out_specs=pl.BlockSpec(memory_space=pltpu.VMEM),
         scratch_shapes=[
+            pltpu.SMEM(bins.shape, jnp.int32),
             pltpu.VMEM(signal.shape, bf16),
             pltpu.VMEM(mic_positions.shape, f32),
             pltpu.VMEM(grid_positions.shape, f32),
@@ -307,9 +325,14 @@
             pltpu.VMEM((groups // X_LO, halves, 128), f32),
             pltpu.VMEM((halves, 128), f32),
             pltpu.VMEM((plane, halves, 128), f32),
+            dma,
             dma((snaps,)),
+            dma,
+            dma,
+            dma,
+            dma((2,)),
         ]
-        + [dma] * 8,
+        + [dma] * 4,
         compiler_params=pltpu.CompilerParams(
             collective_id=0, has_side_effects=True, vmem_limit_bytes=67_043_328
         ),

time: 35.2 us -> 31.4 us (0.89)
  Pallas kernels: 33.7 us -> 29.9 us
    pallas_call x1, Pallas kernels: 33.7 us -> 29.9 us  [shards(): pl.pallas_call(functools.partial(kernel, groups, inners, total_mics), out...]
where the time goes in v2:
time: 31.4 us; the launch traced here: 31.3 us
  Pallas kernels  29.9 us (95%)
  local copies, waits for them, and re-layouts  1.38 us (4%)
    pallas_call x1, Pallas kernels, shards(): pl.pallas_call(functools.partial(kernel, groups, inners, total_mics), out...  29.9 us
    unnamed x1, local copies, waits for them, and re-layouts  1.38 us

profile of v2, /device:TPU:1, one launch (start us, length us, event | category | flops | bytes accessed | tf_op | source)
XLA Modules:
  0.0 31.3 jit_solution(526855988917659068)
XLA Ops:
  0.0 29.9 %beamform.1 = f32[8,1024]{1,0:T(8,128)} custom-call(s32[8]{0:T(128)} %bins_hbm.1, bf16[8,1024,256]{2,1,0:T(8,128)(2,1)} %signal_hbm.1, f32[3,4096]{1,0:T(4,128)} %mic_hbm.1, f32[3,1024]{1,0:T(4,128)} %grid_hbm.1), custom_call_target="tpu_custom_call" | custom-call | tf_op jit(solution)/shard_map/beamform/pallas_call | solution.py:302
  29.9 1.4 %copy.6 = f32[8,1024]{1,0:T(8,128)} copy(f32[8,1024]{1,0:T(8,128)} %beamform.1) | data formatting | bytes 65536
